TPU v7x, 128 devices: a whole 4x4x4 slice. The times are simulated.
128 devices in a mesh: ctx: 16 (over y_hi, z, core), head: 8 (over x, y_lo).
Axes of the slice: x: 4, y: 4 (y_hi: 2, y_lo: 2; y = y_hi * 2 + y_lo), z: 4, core: 2. Of those that a mesh axis runs over, the one named last changes fastest.
Arguments:
- queries: bfloat16 [4096, 8192], P('ctx', 'head'), may hold values from -40 to 40
- keys: bfloat16 [4096, 1024], P('ctx', 'head'), may hold values from -4 to 4
- values: bfloat16 [4096, 1024], P('ctx', 'head'), may hold values from -6 to 6
- out_weight: bfloat16 [8192, 8192], P(None, 'head'), may hold values from -0.1796875 to 0.1796875
- doc_lengths: int32 [16], replicated, may hold values from 1 to 1024, 4096 in all
- owners: int32 [128, 1], replicated, may hold values from 0 to 15; in each aligned block of 8 rows (0 to 7, 8 to 15, ...) no two rows name the same one
Outputs:
- attended: bfloat16 [8192, 8192], P('head', 'ctx')
Inputs may be any that keep to these rules, and one draw needn't show every extreme that they name: `owners`: among the 8 pieces loaded by one index of ctx (aligned blocks of 8 rows) every owner appears at most once. `doc_lengths`: the lengths sum to 4096; the longest is exactly 1024.
All inputs are finite; a program needn't handle non-finite values.
Results may differ from a plain program's by a relative error of at most 0.018.
Values may be sent and summed in bfloat16 or wider, within the bound.
A program may use at most 128 MiB of HBM per device.

v0:
```python
import math
import jax
import jax.numpy as jnp
from jax import lax
from jax.sharding import PartitionSpec as P

HEAD_SIZE = 128
PIECES = 8
MASKED = -1e30


def document_index(positions, doc_starts):
    return jnp.sum((positions[:, None] >= doc_starts[None, :]).astype(jnp.int32), axis=1) - 1


def attend(query_rows, query_pos, keys, values, doc_starts):
    row_count = query_rows.shape[0]
    key_heads = keys.shape[1] // HEAD_SIZE
    group_length = query_rows.shape[1] // keys.shape[1]
    query_heads = query_rows.reshape(row_count, key_heads, group_length, HEAD_SIZE)
    query_doc = document_index(query_pos, doc_starts)
    score_scale = 1.0 / math.sqrt(HEAD_SIZE)
    initial = (
        jnp.full((row_count, key_heads, group_length), MASKED, jnp.float32),
        jnp.zeros((row_count, key_heads, group_length), jnp.float32),
        jnp.zeros((row_count, key_heads, group_length, HEAD_SIZE), jnp.float32),
    )
    key_piece = lax.all_gather(keys, "ctx", axis=0, tiled=True)
    value_piece = lax.all_gather(values, "ctx", axis=0, tiled=True)
    piece_rows = key_piece.shape[0]
    tile_rows = math.gcd(piece_rows, 512)

    def one_tile(tile_index, running):
        tile_start = tile_index * tile_rows
        key_block = lax.dynamic_slice_in_dim(key_piece, tile_start, tile_rows, 0).reshape(
            tile_rows, key_heads, HEAD_SIZE
        )
        value_block = lax.dynamic_slice_in_dim(value_piece, tile_start, tile_rows, 0).reshape(
            tile_rows, key_heads, HEAD_SIZE
        )
        key_pos = tile_start + jnp.arange(tile_rows, dtype=jnp.int32)
        key_doc = document_index(key_pos, doc_starts)
        allowed = (query_doc[:, None] == key_doc[None, :]) & (
            key_pos[None, :] <= query_pos[:, None]
        )
        running_max, running_sum, weighted = running
        scores = (
            jnp.einsum("rkgd,nkd->rkgn", query_heads, key_block, preferred_element_type=jnp.float32)
            * score_scale
        )
        allowed_all = allowed[:, None, None, :]
        scores = jnp.where(allowed_all, scores, MASKED)
        new_max = jnp.maximum(running_max, jnp.max(scores, axis=-1))
        factor = jnp.exp(running_max - new_max)
        weights = jnp.where(allowed_all, jnp.exp(scores - new_max[..., None]), 0.0)
        new_sum = running_sum * factor + jnp.sum(weights, axis=-1)
        new_weighted = weighted * factor[..., None] + jnp.einsum(
            "rkgn,nkd->rkgd",
            weights.astype(jnp.bfloat16),
            value_block,
            preferred_element_type=jnp.float32,
        )
        return (new_max, new_sum, new_weighted)

    final_max, final_sum, weighted = lax.fori_loop(0, piece_rows // tile_rows, one_tile, initial)
    result = weighted / jnp.maximum(final_sum, 1.0)[..., None]
    return result.reshape(row_count, key_heads * group_length * HEAD_SIZE).astype(jnp.bfloat16)


def project(context, out_weight):
    return lax.psum_scatter(
        lax.dot_general(
            out_weight, context, (((1,), (1,)), ((), ())), preferred_element_type=jnp.float32
        ).astype(jnp.bfloat16),
        "head",
        scatter_dimension=0,
        tiled=True,
    )


def per_device(queries, keys, values, out_weight, doc_lengths, owners):
    place_count = lax.axis_size("ctx")
    own_index = lax.axis_index("ctx")
    token_count = queries.shape[0]
    block_rows = token_count // PIECES
    doc_ends = jnp.cumsum(doc_lengths)
    doc_starts = doc_ends - doc_lengths
    owner_table = owners[:, 0].reshape(place_count, PIECES)
    own_owners = lax.dynamic_index_in_dim(owner_table, own_index, 0, keepdims=False)
    place_ids = jnp.arange(place_count, dtype=jnp.int32)
    send_pick = (own_owners[None, :] == place_ids[:, None]).astype(jnp.bfloat16)
    grouped = queries.reshape(PIECES, block_rows, queries.shape[1])
    outgoing = jnp.einsum(
        "oc,chw->ohw", send_pick, grouped, preferred_element_type=jnp.float32
    ).astype(jnp.bfloat16)
    arrived = lax.all_to_all(outgoing, "ctx", split_axis=0, concat_axis=0, tiled=True)
    slot_hits = (owner_table == own_index).astype(jnp.int32)
    slot_live = jnp.sum(slot_hits, axis=1)
    picked = jnp.sum(slot_hits * jnp.arange(PIECES, dtype=jnp.int32)[None, :], axis=1)
    slot_pos = (place_ids[:, None] * PIECES + picked[:, None]) * block_rows + jnp.arange(
        block_rows, dtype=jnp.int32
    )[None, :]
    query_pos = jnp.where(slot_live[:, None] > 0, slot_pos, -1).reshape(-1)
    context = attend(
        arrived.reshape(place_count * block_rows, queries.shape[1]),
        query_pos,
        keys,
        values,
        doc_starts,
    )
    return project(context, out_weight)


def solution(mesh):
    in_specs = (P("ctx", "head"), P("ctx", "head"), P("ctx", "head"), P(None, "head"), P(), P())
    out_specs = P("head", "ctx")
    return jax.shard_map(
        per_device, mesh=mesh, in_specs=in_specs, out_specs=out_specs, check_vma=False
    )
```

profile of v0, /device:TPU:1, one launch (start us, length us, event | category | flops | bytes accessed | tf_op | source)
XLA Modules:
  0.0 447.8 jit_solution(8140803811860141464)
XLA Ops:
  13.0 9.5 %all-to-all-start = ((bf16[16,32,1024]{2,1,0:T(8,128)(2,1)}), bf16[16,32,1024]{2,1,0:T(8,128)(2,1)S(1)}, u32[]{:S(2)}, u32[]{:S(2)}) async-start(bf16[16,32,1024]{2,1,0:T(8,128)(2,1)} %copy.29), calls=%async_computation | async-start | bytes 2097152 | tf_op jit(solution)/shard_map/all_to_all | solution.py:96
  24.5 15.9 %all-to-all-done = bf16[16,32,1024]{2,1,0:T(8,128)(2,1)S(1)} async-done(((bf16[16,32,1024]{2,1,0:T(8,128)(2,1)}), bf16[16,32,1024]{2,1,0:T(8,128)(2,1)S(1)}, u32[]{:S(2)}, u32[]{:S(2)}) %all-to-all-start) | async-done | bytes 1048608 | tf_op jit(solution)/shard_map/all_to_all | solution.py:96
  40.8 20.1 %all-gather.5.cloned.1.call-done = bf16[4096,128]{0,1:T(8,128)(2,1)} async-done(((bf16[256,128]{0,1:T(8,128)(2,1)}), bf16[4096,128]{0,1:T(8,128)(2,1)}) %all-gather.5.cloned.1.call-update) | async-done | bytes 1048592 | tf_op jit(solution)/shard_map/all_gather | solution.py:29
  60.9 47.4 %all-gather.3.cloned.1.call-done = bf16[4096,128]{1,0:T(8,128)(2,1)} async-done(((bf16[256,128]{1,0:T(8,128)(2,1)}), bf16[4096,128]{1,0:T(8,128)(2,1)}) %all-gather.3.cloned.1.call-update) | async-done | bytes 1048592 | tf_op jit(solution)/shard_map/all_gather | solution.py:28
  108.2 131.5 %while.20 = (s32[]{:T(128)}, f32[512,1,8]{0,2,1:T(8,128)S(1)}, f32[512,1,8]{0,2,1:T(8,128)S(1)}, f32[512,1,8,128]{0,3,2,1:T(8,128)}, s32[512]{0:T(512)S(1)}, /*i...) while((s32[]{:T(128)}, f32[512,1,8]{0,2,1:T(8,128)S(1)}, ...), condition=%wide.region_8.9_spmd.clone, body=%wide.region_4.8_spmd.clone.sunk | while | flops 1103414784 | bytes 65560956 | solution.py:65
  108.8 5.6 %fusion.37 = (f32[512,8]{0,1:T(8,128)S(1)}, f32[512,512,8]{1,0,2:T(8,128)}) fusion(pred[512,512]{0,1:T(8,128)(4,1)S(1)} %compare_and_fusion.2, bf16[512,1,8,128]{3,0,2,1:T(8,128)(2,1)S(1)} %get-tuple-element.463, bf16[4096,128]{1,0:T(8,128)(2,1)} %get-tuple-element.462, s32[]{:T(128)S(6)} %select_n.96), kind=kOutput, calls=%fused_computation.3.clone.1 | convolution fusion | flops 543158272 | bytes 9846788 | tf_op jit(solution)/shard_map/while/body/eval_jaxpr/rkgd,nkd->rkgn/dot_general | solution.py:48
  114.4 7.6 %bitcast_add_fusion.5 = f32[512,1,8,128]{0,3,2,1:T(8,128)} fusion(f32[512,1,8,128]{0,3,2,1:T(8,128)} %get-tuple-element.444, f32[512,512,8]{1,0,2:T(8,128)} %get-tuple-element.424, f32[512,8]{0,1:T(8,128)S(1)} %bitcast.90, pred[512,512]{0,1:T(8,128)(4,1)S(1)} %compare_and_fusion.2, f32[512,8]{0,1:T(8,128)S(1)} %get-tuple-element.425, ...), kind=kOutput, calls=%fused_computation.9.clone.1 | convolution fusion | flops 548929536 | bytes 13008901 | tf_op jit(solution)/shard_map/while/body/eval_jaxpr/rkgn,nkd->rkgd/dot_general | solution.py:57
  122.1 2.0 fusion.39
  124.7 5.6 %fusion.37 = (f32[512,8]{0,1:T(8,128)S(1)}, f32[512,512,8]{1,0,2:T(8,128)}) fusion(pred[512,512]{0,1:T(8,128)(4,1)S(1)} %compare_and_fusion.2, bf16[512,1,8,128]{3,0,2,1:T(8,128)(2,1)S(1)} %get-tuple-element.463, bf16[4096,128]{1,0:T(8,128)(2,1)} %get-tuple-element.462, s32[]{:T(128)S(6)} %select_n.96), kind=kOutput, calls=%fused_computation.3.clone.1 | convolution fusion | flops 543158272 | bytes 9846788 | tf_op jit(solution)/shard_map/while/body/eval_jaxpr/rkgd,nkd->rkgn/dot_general | solution.py:48
  130.3 8.2 %bitcast_add_fusion.5 = f32[512,1,8,128]{0,3,2,1:T(8,128)} fusion(f32[512,1,8,128]{0,3,2,1:T(8,128)} %get-tuple-element.444, f32[512,512,8]{1,0,2:T(8,128)} %get-tuple-element.424, f32[512,8]{0,1:T(8,128)S(1)} %bitcast.90, pred[512,512]{0,1:T(8,128)(4,1)S(1)} %compare_and_fusion.2, f32[512,8]{0,1:T(8,128)S(1)} %get-tuple-element.425, ...), kind=kOutput, calls=%fused_computation.9.clone.1 | convolution fusion | flops 548929536 | bytes 13008901 | tf_op jit(solution)/shard_map/while/body/eval_jaxpr/rkgn,nkd->rkgd/dot_general | solution.py:57
  138.6 2.0 fusion.39
  141.2 5.6 %fusion.37 = (f32[512,8]{0,1:T(8,128)S(1)}, f32[512,512,8]{1,0,2:T(8,128)}) fusion(pred[512,512]{0,1:T(8,128)(4,1)S(1)} %compare_and_fusion.2, bf16[512,1,8,128]{3,0,2,1:T(8,128)(2,1)S(1)} %get-tuple-element.463, bf16[4096,128]{1,0:T(8,128)(2,1)} %get-tuple-element.462, s32[]{:T(128)S(6)} %select_n.96), kind=kOutput, calls=%fused_computation.3.clone.1 | convolution fusion | flops 543158272 | bytes 9846788 | tf_op jit(solution)/shard_map/while/body/eval_jaxpr/rkgd,nkd->rkgn/dot_general | solution.py:48
  146.8 8.2 %bitcast_add_fusion.5 = f32[512,1,8,128]{0,3,2,1:T(8,128)} fusion(f32[512,1,8,128]{0,3,2,1:T(8,128)} %get-tuple-element.444, f32[512,512,8]{1,0,2:T(8,128)} %get-tuple-element.424, f32[512,8]{0,1:T(8,128)S(1)} %bitcast.90, pred[512,512]{0,1:T(8,128)(4,1)S(1)} %compare_and_fusion.2, f32[512,8]{0,1:T(8,128)S(1)} %get-tuple-element.425, ...), kind=kOutput, calls=%fused_computation.9.clone.1 | convolution fusion | flops 548929536 | bytes 13008901 | tf_op jit(solution)/shard_map/while/body/eval_jaxpr/rkgn,nkd->rkgd/dot_general | solution.py:57
  155.1 2.0 fusion.39
  157.7 5.6 %fusion.37 = (f32[512,8]{0,1:T(8,128)S(1)}, f32[512,512,8]{1,0,2:T(8,128)}) fusion(pred[512,512]{0,1:T(8,128)(4,1)S(1)} %compare_and_fusion.2, bf16[512,1,8,128]{3,0,2,1:T(8,128)(2,1)S(1)} %get-tuple-element.463, bf16[4096,128]{1,0:T(8,128)(2,1)} %get-tuple-element.462, s32[]{:T(128)S(6)} %select_n.96), kind=kOutput, calls=%fused_computation.3.clone.1 | convolution fusion | flops 543158272 | bytes 9846788 | tf_op jit(solution)/shard_map/while/body/eval_jaxpr/rkgd,nkd->rkgn/dot_general | solution.py:48
  163.3 8.2 %bitcast_add_fusion.5 = f32[512,1,8,128]{0,3,2,1:T(8,128)} fusion(f32[512,1,8,128]{0,3,2,1:T(8,128)} %get-tuple-element.444, f32[512,512,8]{1,0,2:T(8,128)} %get-tuple-element.424, f32[512,8]{0,1:T(8,128)S(1)} %bitcast.90, pred[512,512]{0,1:T(8,128)(4,1)S(1)} %compare_and_fusion.2, f32[512,8]{0,1:T(8,128)S(1)} %get-tuple-element.425, ...), kind=kOutput, calls=%fused_computation.9.clone.1 | convolution fusion | flops 548929536 | bytes 13008901 | tf_op jit(solution)/shard_map/while/body/eval_jaxpr/rkgn,nkd->rkgd/dot_general | solution.py:57
  171.6 2.0 fusion.39
  174.2 5.6 %fusion.37 = (f32[512,8]{0,1:T(8,128)S(1)}, f32[512,512,8]{1,0,2:T(8,128)}) fusion(pred[512,512]{0,1:T(8,128)(4,1)S(1)} %compare_and_fusion.2, bf16[512,1,8,128]{3,0,2,1:T(8,128)(2,1)S(1)} %get-tuple-element.463, bf16[4096,128]{1,0:T(8,128)(2,1)} %get-tuple-element.462, s32[]{:T(128)S(6)} %select_n.96), kind=kOutput, calls=%fused_computation.3.clone.1 | convolution fusion | flops 543158272 | bytes 9846788 | tf_op jit(solution)/shard_map/while/body/eval_jaxpr/rkgd,nkd->rkgn/dot_general | solution.py:48
  179.9 8.2 %bitcast_add_fusion.5 = f32[512,1,8,128]{0,3,2,1:T(8,128)} fusion(f32[512,1,8,128]{0,3,2,1:T(8,128)} %get-tuple-element.444, f32[512,512,8]{1,0,2:T(8,128)} %get-tuple-element.424, f32[512,8]{0,1:T(8,128)S(1)} %bitcast.90, pred[512,512]{0,1:T(8,128)(4,1)S(1)} %compare_and_fusion.2, f32[512,8]{0,1:T(8,128)S(1)} %get-tuple-element.425, ...), kind=kOutput, calls=%fused_computation.9.clone.1 | convolution fusion | flops 548929536 | bytes 13008901 | tf_op jit(solution)/shard_map/while/body/eval_jaxpr/rkgn,nkd->rkgd/dot_general | solution.py:57
  188.1 2.0 fusion.39
  190.7 5.6 %fusion.37 = (f32[512,8]{0,1:T(8,128)S(1)}, f32[512,512,8]{1,0,2:T(8,128)}) fusion(pred[512,512]{0,1:T(8,128)(4,1)S(1)} %compare_and_fusion.2, bf16[512,1,8,128]{3,0,2,1:T(8,128)(2,1)S(1)} %get-tuple-element.463, bf16[4096,128]{1,0:T(8,128)(2,1)} %get-tuple-element.462, s32[]{:T(128)S(6)} %select_n.96), kind=kOutput, calls=%fused_computation.3.clone.1 | convolution fusion | flops 543158272 | bytes 9846788 | tf_op jit(solution)/shard_map/while/body/eval_jaxpr/rkgd,nkd->rkgn/dot_general | solution.py:48
  196.4 8.2 %bitcast_add_fusion.5 = f32[512,1,8,128]{0,3,2,1:T(8,128)} fusion(f32[512,1,8,128]{0,3,2,1:T(8,128)} %get-tuple-element.444, f32[512,512,8]{1,0,2:T(8,128)} %get-tuple-element.424, f32[512,8]{0,1:T(8,128)S(1)} %bitcast.90, pred[512,512]{0,1:T(8,128)(4,1)S(1)} %compare_and_fusion.2, f32[512,8]{0,1:T(8,128)S(1)} %get-tuple-element.425, ...), kind=kOutput, calls=%fused_computation.9.clone.1 | convolution fusion | flops 548929536 | bytes 13008901 | tf_op jit(solution)/shard_map/while/body/eval_jaxpr/rkgn,nkd->rkgd/dot_general | solution.py:57
  204.6 2.0 fusion.39
  207.2 5.6 %fusion.37 = (f32[512,8]{0,1:T(8,128)S(1)}, f32[512,512,8]{1,0,2:T(8,128)}) fusion(pred[512,512]{0,1:T(8,128)(4,1)S(1)} %compare_and_fusion.2, bf16[512,1,8,128]{3,0,2,1:T(8,128)(2,1)S(1)} %get-tuple-element.463, bf16[4096,128]{1,0:T(8,128)(2,1)} %get-tuple-element.462, s32[]{:T(128)S(6)} %select_n.96), kind=kOutput, calls=%fused_computation.3.clone.1 | convolution fusion | flops 543158272 | bytes 9846788 | tf_op jit(solution)/shard_map/while/body/eval_jaxpr/rkgd,nkd->rkgn/dot_general | solution.py:48
  212.9 8.2 %bitcast_add_fusion.5 = f32[512,1,8,128]{0,3,2,1:T(8,128)} fusion(f32[512,1,8,128]{0,3,2,1:T(8,128)} %get-tuple-element.444, f32[512,512,8]{1,0,2:T(8,128)} %get-tuple-element.424, f32[512,8]{0,1:T(8,128)S(1)} %bitcast.90, pred[512,512]{0,1:T(8,128)(4,1)S(1)} %compare_and_fusion.2, f32[512,8]{0,1:T(8,128)S(1)} %get-tuple-element.425, ...), kind=kOutput, calls=%fused_computation.9.clone.1 | convolution fusion | flops 548929536 | bytes 13008901 | tf_op jit(solution)/shard_map/while/body/eval_jaxpr/rkgn,nkd->rkgd/dot_general | solution.py:57
  221.1 2.0 fusion.39
  223.8 5.6 %fusion.37 = (f32[512,8]{0,1:T(8,128)S(1)}, f32[512,512,8]{1,0,2:T(8,128)}) fusion(pred[512,512]{0,1:T(8,128)(4,1)S(1)} %compare_and_fusion.2, bf16[512,1,8,128]{3,0,2,1:T(8,128)(2,1)S(1)} %get-tuple-element.463, bf16[4096,128]{1,0:T(8,128)(2,1)} %get-tuple-element.462, s32[]{:T(128)S(6)} %select_n.96), kind=kOutput, calls=%fused_computation.3.clone.1 | convolution fusion | flops 543158272 | bytes 9846788 | tf_op jit(solution)/shard_map/while/body/eval_jaxpr/rkgd,nkd->rkgn/dot_general | solution.py:48
  229.4 8.2 %bitcast_add_fusion.5 = f32[512,1,8,128]{0,3,2,1:T(8,128)} fusion(f32[512,1,8,128]{0,3,2,1:T(8,128)} %get-tuple-element.444, f32[512,512,8]{1,0,2:T(8,128)} %get-tuple-element.424, f32[512,8]{0,1:T(8,128)S(1)} %bitcast.90, pred[512,512]{0,1:T(8,128)(4,1)S(1)} %compare_and_fusion.2, f32[512,8]{0,1:T(8,128)S(1)} %get-tuple-element.425, ...), kind=kOutput, calls=%fused_computation.9.clone.1 | convolution fusion | flops 548929536 | bytes 13008901 | tf_op jit(solution)/shard_map/while/body/eval_jaxpr/rkgn,nkd->rkgd/dot_general | solution.py:57
  237.7 2.0 fusion.39
  241.6 29.8 %fusion.23 = bf16[8192,512]{0,1:T(8,128)(2,1)} fusion(bf16[512,1024]{0,1:T(8,128)(2,1)S(1)} %bitcast.94, bf16[8192,1024]{1,0:T(8,128)(2,1)} %param.11), kind=kOutput, calls=%fused_computation.33 | convolution fusion | flops 8594128896 | bytes 26214400 | tf_op jit(solution)/shard_map/dot_general | solution.py:72
  271.5 167.6 %reduce-scatter.2.cloned.1.call-done = bf16[1024,512]{0,1:T(8,128)(2,1)} async-done(((bf16[8192,512]{0,1:T(8,128)(2,1)}), bf16[1024,512]{0,1:T(8,128)(2,1)}) %reduce-scatter.2.cloned.1.call-update) | async-done | bytes 1048592 | tf_op jit(solution)/shard_map/reduce_scatter | solution.py:71
  439.0 2.3 copy.32
  (121 shorter events, 15.2 us)
Async XLA Ops:
  6.5 4.3 copy-start
  6.5 54.3 %all-gather.5.cloned.1.call-start = ((), (), s32[]{:S(2)}) async-start(), calls=%async_computation.3 | async-start | bytes 1114112 | tf_op jit(solution)/shard_map/all_gather | solution.py:29
  8.2 100.0 %all-gather.3.cloned.1.call-start = ((), (), s32[]{:S(2)}) async-start(), calls=%async_computation.2 | async-start | bytes 1114112 | tf_op jit(solution)/shard_map/all_gather | solution.py:28
  13.0 27.4 %all-to-all-start = ((bf16[16,32,1024]{2,1,0:T(8,128)(2,1)}), bf16[16,32,1024]{2,1,0:T(8,128)(2,1)S(1)}, u32[]{:S(2)}, u32[]{:S(2)}) async-start(bf16[16,32,1024]{2,1,0:T(8,128)(2,1)} %copy.29), calls=%async_computation | async-start | bytes 2097152 | tf_op jit(solution)/shard_map/all_to_all | solution.py:96
  22.5 416.6 %reduce-scatter.2.cloned.1.call-start = ((), (), s32[]{:S(2)}) async-start(), calls=%async_computation.4 | async-start | bytes 9437184 | tf_op jit(solution)/shard_map/reduce_scatter | solution.py:71
  114.4 7.7 %copy-start.1 = (f32[512,512,8]{1,0,2:T(8,128)S(1)}, f32[512,512,8]{1,0,2:T(8,128)}, u32[]{:S(2)}) copy-start(f32[512,512,8]{1,0,2:T(8,128)} %get-tuple-element.424) | copy-start | bytes 25165828 | tf_op jit(solution)/shard_map/while
  130.3 8.3 %copy-start.1 = (f32[512,512,8]{1,0,2:T(8,128)S(1)}, f32[512,512,8]{1,0,2:T(8,128)}, u32[]{:S(2)}) copy-start(f32[512,512,8]{1,0,2:T(8,128)} %get-tuple-element.424) | copy-start | bytes 25165828 | tf_op jit(solution)/shard_map/while
  146.8 8.3 %copy-start.1 = (f32[512,512,8]{1,0,2:T(8,128)S(1)}, f32[512,512,8]{1,0,2:T(8,128)}, u32[]{:S(2)}) copy-start(f32[512,512,8]{1,0,2:T(8,128)} %get-tuple-element.424) | copy-start | bytes 25165828 | tf_op jit(solution)/shard_map/while
  163.3 8.3 %copy-start.1 = (f32[512,512,8]{1,0,2:T(8,128)S(1)}, f32[512,512,8]{1,0,2:T(8,128)}, u32[]{:S(2)}) copy-start(f32[512,512,8]{1,0,2:T(8,128)} %get-tuple-element.424) | copy-start | bytes 25165828 | tf_op jit(solution)/shard_map/while
  179.8 8.3 %copy-start.1 = (f32[512,512,8]{1,0,2:T(8,128)S(1)}, f32[512,512,8]{1,0,2:T(8,128)}, u32[]{:S(2)}) copy-start(f32[512,512,8]{1,0,2:T(8,128)} %get-tuple-element.424) | copy-start | bytes 25165828 | tf_op jit(solution)/shard_map/while
  196.4 8.3 %copy-start.1 = (f32[512,512,8]{1,0,2:T(8,128)S(1)}, f32[512,512,8]{1,0,2:T(8,128)}, u32[]{:S(2)}) copy-start(f32[512,512,8]{1,0,2:T(8,128)} %get-tuple-element.424) | copy-start | bytes 25165828 | tf_op jit(solution)/shard_map/while
  212.9 8.3 %copy-start.1 = (f32[512,512,8]{1,0,2:T(8,128)S(1)}, f32[512,512,8]{1,0,2:T(8,128)}, u32[]{:S(2)}) copy-start(f32[512,512,8]{1,0,2:T(8,128)} %get-tuple-element.424) | copy-start | bytes 25165828 | tf_op jit(solution)/shard_map/while
  229.4 8.3 %copy-start.1 = (f32[512,512,8]{1,0,2:T(8,128)S(1)}, f32[512,512,8]{1,0,2:T(8,128)}, u32[]{:S(2)}) copy-start(f32[512,512,8]{1,0,2:T(8,128)} %get-tuple-element.424) | copy-start | bytes 25165828 | tf_op jit(solution)/shard_map/while
Sparse Core Ops, SparseCore 0:
  9.6 51.1 all-gather.4
  63.3 44.8 all-gather.2
  271.6 167.4 reduce-scatter.1
where the time goes:
time: 448 us
  waiting for transfers between devices  252 us (56%)
  matrix products  141 us (31%)
  other arithmetic  24.2 us (5%)
  between operations  13.2 us (3%)
  starting transfers between devices  9.54 us (2%)
  local copies, waits for them, and re-layouts  7.97 us (2%)
    reduce_scatter x1, waiting for transfers between devices, project(): lax.psum_scatter(lax.dot_general(out_weight, context, (((1,), (1,)), ((),...  168 us
    dot_general x8, matrix products, one_tile(): jnp.einsum('rkgn,nkd->rkgd', weights.astype(jnp.bfloat16), value_block, p...  65.4 us
    all_gather x1, waiting for transfers between devices, attend(): key_piece = lax.all_gather(keys, 'ctx', axis=0, tiled=True)  47.4 us
    dot_general x8, matrix products, one_tile(): jnp.einsum('rkgd,nkd->rkgn', query_heads, key_block, preferred_element_ty...  44.9 us
    dot_general x1, matrix products, project(): lax.dot_general(out_weight, context, (((1,), (1,)), ((), ())), preferred_...  29.8 us
    all_gather x1, waiting for transfers between devices, attend(): value_piece = lax.all_gather(values, 'ctx', axis=0, tiled=True)  20.1 us
    reduce_sum x8, other arithmetic, one_tile(): new_sum = running_sum * factor + jnp.sum(weights, axis=-1)  16.1 us
    all_to_all x1, waiting for transfers between devices, per_device(): lax.all_to_all(outgoing, 'ctx', split_axis=0, concat_axis=0, tiled=True)  15.9 us
  transfers between devices with their start and end apart: 4, of which 4 were waited for; matrix products, arithmetic and copies ran while one was open for 1% of the time, Pallas kernels for 0%

commit v1 on v0

--- a/solution.py
+++ b/solution.py
@@ -26,7 +26,9 @@
         jnp.zeros((row_count, key_heads, group_length, HEAD_SIZE), jnp.float32),
     )
     key_piece = lax.all_gather(keys, "ctx", axis=0, tiled=True)
-    value_piece = lax.all_gather(values, "ctx", axis=0, tiled=True)
+    value_piece = jnp.concatenate(
+        lax.all_to_all(jnp.stack([values] * lax.axis_size("ctx")), "ctx", 0, 0), axis=0
+    )
     piece_rows = key_piece.shape[0]
     tile_rows = math.gcd(piece_rows, 512)
 

time: 448 us -> 410 us (0.915)
  waiting for transfers between devices: 252 us -> 209 us
    all_gather x1, waiting for transfers between devices: 47.4 us -> 8.56 us  [attend(): key_piece = lax.all_gather(keys, 'ctx', axis=0, tiled=True)]
    all_gather x1 -> x0, waiting for transfers between devices: 20.1 us -> none  [attend(): value_piece = lax.all_gather(values, 'ctx', axis=0, tiled=True)]
    all_to_all x0 -> x1, waiting for transfers between devices: none -> 16.3 us  [attend(): lax.all_to_all(jnp.stack([values] * lax.axis_size('ctx')), 'ctx', 0, 0)]
where the time goes in v1:
time: 410 us; the launch traced here: 409 us
  waiting for transfers between devices  209 us (51%)
  matrix products  140 us (34%)
  other arithmetic  23.6 us (6%)
  starting transfers between devices  13.9 us (3%)
  between operations  13.5 us (3%)
  local copies, waits for them, and re-layouts  9.02 us (2%)
    reduce_scatter x1, waiting for transfers between devices, project(): lax.psum_scatter(lax.dot_general(out_weight, context, (((1,), (1,)), ((),...  168 us
    dot_general x8, matrix products, one_tile(): jnp.einsum('rkgn,nkd->rkgd', weights.astype(jnp.bfloat16), value_block, p...  64.8 us
    dot_general x8, matrix products, one_tile(): jnp.einsum('rkgd,nkd->rkgn', query_heads, key_block, preferred_element_ty...  44.9 us
    dot_general x1, matrix products, project(): lax.dot_general(out_weight, context, (((1,), (1,)), ((), ())), preferred_...  29.8 us
    all_to_all x1, waiting for transfers between devices, attend(): lax.all_to_all(jnp.stack([values] * lax.axis_size('ctx')), 'ctx', 0, 0)  16.3 us
    reduce_sum x8, other arithmetic, one_tile(): new_sum = running_sum * factor + jnp.sum(weights, axis=-1)  16.1 us
    all_to_all x1, waiting for transfers between devices, per_device(): lax.all_to_all(outgoing, 'ctx', split_axis=0, concat_axis=0, tiled=True)  15.4 us
    all_to_all x1, starting transfers between devices, per_device(): lax.all_to_all(outgoing, 'ctx', split_axis=0, concat_axis=0, tiled=True)  9.46 us
  transfers between devices with their start and end apart: 4, of which 4 were waited for; matrix products, arithmetic and copies ran while one was open for 1% of the time, Pallas kernels for 0%

profile of v1, /device:TPU:1, one launch (start us, length us, event | category | flops | bytes accessed | tf_op | source)
XLA Modules:
  0.0 409.3 jit_solution(2171669119722088840)
XLA Ops:
  10.6 9.5 %all-to-all-start = ((bf16[16,32,1024]{2,1,0:T(8,128)(2,1)}), bf16[16,32,1024]{2,1,0:T(8,128)(2,1)S(1)}, u32[]{:S(2)}, u32[]{:S(2)}) async-start(bf16[16,32,1024]{2,1,0:T(8,128)(2,1)} %copy.38), calls=%async_computation | async-start | bytes 2097152 | tf_op jit(solution)/shard_map/all_to_all | solution.py:98
  21.9 15.4 %all-to-all-done = bf16[16,32,1024]{2,1,0:T(8,128)(2,1)S(1)} async-done(((bf16[16,32,1024]{2,1,0:T(8,128)(2,1)}), bf16[16,32,1024]{2,1,0:T(8,128)(2,1)S(1)}, u32[]{:S(2)}, u32[]{:S(2)}) %all-to-all-start) | async-done | bytes 1048608 | tf_op jit(solution)/shard_map/all_to_all | solution.py:98
  38.3 4.4 %all-to-all-start.1 = ((bf16[16,256,128]{1,2,0:T(8,128)(2,1)}), bf16[16,256,128]{1,2,0:T(8,128)(2,1)S(1)}, u32[]{:S(2)}, u32[]{:S(2)}) async-start(bf16[16,256,128]{1,2,0:T(8,128)(2,1)} %stack.2), calls=%async_computation.1 | async-start | bytes 2097152 | tf_op jit(solution)/shard_map/all_to_all | solution.py:30
  43.7 16.3 %all-to-all-done.1 = bf16[16,256,128]{1,2,0:T(8,128)(2,1)S(1)} async-done(((bf16[16,256,128]{1,2,0:T(8,128)(2,1)}), bf16[16,256,128]{1,2,0:T(8,128)(2,1)S(1)}, u32[]{:S(2)}, u32[]{:S(2)}) %all-to-all-start.1) | async-done | bytes 1048608 | tf_op jit(solution)/shard_map/all_to_all | solution.py:30
  61.3 8.6 %all-gather.2.cloned.1.call-done = bf16[4096,128]{1,0:T(8,128)(2,1)} async-done(((bf16[256,128]{1,0:T(8,128)(2,1)}), bf16[4096,128]{1,0:T(8,128)(2,1)}) %all-gather.2.cloned.1.call-update) | async-done | bytes 1048592 | tf_op jit(solution)/shard_map/all_gather | solution.py:28
  69.9 130.9 %while.20 = (s32[]{:T(128)}, f32[512,1,8]{0,2,1:T(8,128)S(1)}, f32[512,1,8]{0,2,1:T(8,128)S(1)}, f32[512,1,8,128]{0,3,2,1:T(8,128)}, s32[512]{0:T(512)S(1)}, /*i...) while((s32[]{:T(128)}, f32[512,1,8]{0,2,1:T(8,128)S(1)}, ...), condition=%wide.region_8.9_spmd.clone, body=%wide.region_4.8_spmd.clone.sunk | while | flops 1103414784 | bytes 65560956 | solution.py:67
  70.4 5.6 %fusion.37 = (f32[512,8]{0,1:T(8,128)S(1)}, f32[512,512,8]{1,0,2:T(8,128)}) fusion(pred[512,512]{0,1:T(8,128)(4,1)S(1)} %compare_and_fusion.2, bf16[512,1,8,128]{3,0,2,1:T(8,128)(2,1)S(1)} %get-tuple-element.474, bf16[4096,128]{1,0:T(8,128)(2,1)} %get-tuple-element.473, s32[]{:T(128)S(6)} %select_n.96), kind=kOutput, calls=%fused_computation.3.clone.1 | convolution fusion | flops 543158272 | bytes 9846788 | tf_op jit(solution)/shard_map/while/body/eval_jaxpr/rkgd,nkd->rkgn/dot_general | solution.py:50
  76.0 7.6 %bitcast_add_fusion.5 = f32[512,1,8,128]{0,3,2,1:T(8,128)} fusion(f32[512,1,8,128]{0,3,2,1:T(8,128)} %get-tuple-element.455, f32[512,512,8]{1,0,2:T(8,128)} %get-tuple-element.435, f32[512,8]{0,1:T(8,128)S(1)} %bitcast.92, pred[512,512]{0,1:T(8,128)(4,1)S(1)} %compare_and_fusion.2, f32[512,8]{0,1:T(8,128)S(1)} %get-tuple-element.436, ...), kind=kOutput, calls=%fused_computation.9.clone.1 | convolution fusion | flops 548929536 | bytes 13008901 | tf_op jit(solution)/shard_map/while/body/eval_jaxpr/rkgn,nkd->rkgd/dot_general | solution.py:59
  83.6 2.0 fusion.39
  86.3 5.6 %fusion.37 = (f32[512,8]{0,1:T(8,128)S(1)}, f32[512,512,8]{1,0,2:T(8,128)}) fusion(pred[512,512]{0,1:T(8,128)(4,1)S(1)} %compare_and_fusion.2, bf16[512,1,8,128]{3,0,2,1:T(8,128)(2,1)S(1)} %get-tuple-element.474, bf16[4096,128]{1,0:T(8,128)(2,1)} %get-tuple-element.473, s32[]{:T(128)S(6)} %select_n.96), kind=kOutput, calls=%fused_computation.3.clone.1 | convolution fusion | flops 543158272 | bytes 9846788 | tf_op jit(solution)/shard_map/while/body/eval_jaxpr/rkgd,nkd->rkgn/dot_general | solution.py:50
  91.9 8.2 %bitcast_add_fusion.5 = f32[512,1,8,128]{0,3,2,1:T(8,128)} fusion(f32[512,1,8,128]{0,3,2,1:T(8,128)} %get-tuple-element.455, f32[512,512,8]{1,0,2:T(8,128)} %get-tuple-element.435, f32[512,8]{0,1:T(8,128)S(1)} %bitcast.92, pred[512,512]{0,1:T(8,128)(4,1)S(1)} %compare_and_fusion.2, f32[512,8]{0,1:T(8,128)S(1)} %get-tuple-element.436, ...), kind=kOutput, calls=%fused_computation.9.clone.1 | convolution fusion | flops 548929536 | bytes 13008901 | tf_op jit(solution)/shard_map/while/body/eval_jaxpr/rkgn,nkd->rkgd/dot_general | solution.py:59
  100.1 2.0 fusion.39
  102.7 5.6 %fusion.37 = (f32[512,8]{0,1:T(8,128)S(1)}, f32[512,512,8]{1,0,2:T(8,128)}) fusion(pred[512,512]{0,1:T(8,128)(4,1)S(1)} %compare_and_fusion.2, bf16[512,1,8,128]{3,0,2,1:T(8,128)(2,1)S(1)} %get-tuple-element.474, bf16[4096,128]{1,0:T(8,128)(2,1)} %get-tuple-element.473, s32[]{:T(128)S(6)} %select_n.96), kind=kOutput, calls=%fused_computation.3.clone.1 | convolution fusion | flops 543158272 | bytes 9846788 | tf_op jit(solution)/shard_map/while/body/eval_jaxpr/rkgd,nkd->rkgn/dot_general | solution.py:50
  108.3 8.2 %bitcast_add_fusion.5 = f32[512,1,8,128]{0,3,2,1:T(8,128)} fusion(f32[512,1,8,128]{0,3,2,1:T(8,128)} %get-tuple-element.455, f32[512,512,8]{1,0,2:T(8,128)} %get-tuple-element.435, f32[512,8]{0,1:T(8,128)S(1)} %bitcast.92, pred[512,512]{0,1:T(8,128)(4,1)S(1)} %compare_and_fusion.2, f32[512,8]{0,1:T(8,128)S(1)} %get-tuple-element.436, ...), kind=kOutput, calls=%fused_computation.9.clone.1 | convolution fusion | flops 548929536 | bytes 13008901 | tf_op jit(solution)/shard_map/while/body/eval_jaxpr/rkgn,nkd->rkgd/dot_general | solution.py:59
  116.5 2.0 fusion.39
  119.1 5.6 %fusion.37 = (f32[512,8]{0,1:T(8,128)S(1)}, f32[512,512,8]{1,0,2:T(8,128)}) fusion(pred[512,512]{0,1:T(8,128)(4,1)S(1)} %compare_and_fusion.2, bf16[512,1,8,128]{3,0,2,1:T(8,128)(2,1)S(1)} %get-tuple-element.474, bf16[4096,128]{1,0:T(8,128)(2,1)} %get-tuple-element.473, s32[]{:T(128)S(6)} %select_n.96), kind=kOutput, calls=%fused_computation.3.clone.1 | convolution fusion | flops 543158272 | bytes 9846788 | tf_op jit(solution)/shard_map/while/body/eval_jaxpr/rkgd,nkd->rkgn/dot_general | solution.py:50
  124.8 8.2 %bitcast_add_fusion.5 = f32[512,1,8,128]{0,3,2,1:T(8,128)} fusion(f32[512,1,8,128]{0,3,2,1:T(8,128)} %get-tuple-element.455, f32[512,512,8]{1,0,2:T(8,128)} %get-tuple-element.435, f32[512,8]{0,1:T(8,128)S(1)} %bitcast.92, pred[512,512]{0,1:T(8,128)(4,1)S(1)} %compare_and_fusion.2, f32[512,8]{0,1:T(8,128)S(1)} %get-tuple-element.436, ...), kind=kOutput, calls=%fused_computation.9.clone.1 | convolution fusion | flops 548929536 | bytes 13008901 | tf_op jit(solution)/shard_map/while/body/eval_jaxpr/rkgn,nkd->rkgd/dot_general | solution.py:59
  132.9 2.0 fusion.39
  135.6 5.6 %fusion.37 = (f32[512,8]{0,1:T(8,128)S(1)}, f32[512,512,8]{1,0,2:T(8,128)}) fusion(pred[512,512]{0,1:T(8,128)(4,1)S(1)} %compare_and_fusion.2, bf16[512,1,8,128]{3,0,2,1:T(8,128)(2,1)S(1)} %get-tuple-element.474, bf16[4096,128]{1,0:T(8,128)(2,1)} %get-tuple-element.473, s32[]{:T(128)S(6)} %select_n.96), kind=kOutput, calls=%fused_computation.3.clone.1 | convolution fusion | flops 543158272 | bytes 9846788 | tf_op jit(solution)/shard_map/while/body/eval_jaxpr/rkgd,nkd->rkgn/dot_general | solution.py:50
  141.2 8.2 %bitcast_add_fusion.5 = f32[512,1,8,128]{0,3,2,1:T(8,128)} fusion(f32[512,1,8,128]{0,3,2,1:T(8,128)} %get-tuple-element.455, f32[512,512,8]{1,0,2:T(8,128)} %get-tuple-element.435, f32[512,8]{0,1:T(8,128)S(1)} %bitcast.92, pred[512,512]{0,1:T(8,128)(4,1)S(1)} %compare_and_fusion.2, f32[512,8]{0,1:T(8,128)S(1)} %get-tuple-element.436, ...), kind=kOutput, calls=%fused_computation.9.clone.1 | convolution fusion | flops 548929536 | bytes 13008901 | tf_op jit(solution)/shard_map/while/body/eval_jaxpr/rkgn,nkd->rkgd/dot_general | solution.py:59
  149.4 2.0 fusion.39
  152.0 5.6 %fusion.37 = (f32[512,8]{0,1:T(8,128)S(1)}, f32[512,512,8]{1,0,2:T(8,128)}) fusion(pred[512,512]{0,1:T(8,128)(4,1)S(1)} %compare_and_fusion.2, bf16[512,1,8,128]{3,0,2,1:T(8,128)(2,1)S(1)} %get-tuple-element.474, bf16[4096,128]{1,0:T(8,128)(2,1)} %get-tuple-element.473, s32[]{:T(128)S(6)} %select_n.96), kind=kOutput, calls=%fused_computation.3.clone.1 | convolution fusion | flops 543158272 | bytes 9846788 | tf_op jit(solution)/shard_map/while/body/eval_jaxpr/rkgd,nkd->rkgn/dot_general | solution.py:50
  157.6 8.2 %bitcast_add_fusion.5 = f32[512,1,8,128]{0,3,2,1:T(8,128)} fusion(f32[512,1,8,128]{0,3,2,1:T(8,128)} %get-tuple-element.455, f32[512,512,8]{1,0,2:T(8,128)} %get-tuple-element.435, f32[512,8]{0,1:T(8,128)S(1)} %bitcast.92, pred[512,512]{0,1:T(8,128)(4,1)S(1)} %compare_and_fusion.2, f32[512,8]{0,1:T(8,128)S(1)} %get-tuple-element.436, ...), kind=kOutput, calls=%fused_computation.9.clone.1 | convolution fusion | flops 548929536 | bytes 13008901 | tf_op jit(solution)/shard_map/while/body/eval_jaxpr/rkgn,nkd->rkgd/dot_general | solution.py:59
  165.8 2.0 fusion.39
  168.4 5.6 %fusion.37 = (f32[512,8]{0,1:T(8,128)S(1)}, f32[512,512,8]{1,0,2:T(8,128)}) fusion(pred[512,512]{0,1:T(8,128)(4,1)S(1)} %compare_and_fusion.2, bf16[512,1,8,128]{3,0,2,1:T(8,128)(2,1)S(1)} %get-tuple-element.474, bf16[4096,128]{1,0:T(8,128)(2,1)} %get-tuple-element.473, s32[]{:T(128)S(6)} %select_n.96), kind=kOutput, calls=%fused_computation.3.clone.1 | convolution fusion | flops 543158272 | bytes 9846788 | tf_op jit(solution)/shard_map/while/body/eval_jaxpr/rkgd,nkd->rkgn/dot_general | solution.py:50
  174.1 8.2 %bitcast_add_fusion.5 = f32[512,1,8,128]{0,3,2,1:T(8,128)} fusion(f32[512,1,8,128]{0,3,2,1:T(8,128)} %get-tuple-element.455, f32[512,512,8]{1,0,2:T(8,128)} %get-tuple-element.435, f32[512,8]{0,1:T(8,128)S(1)} %bitcast.92, pred[512,512]{0,1:T(8,128)(4,1)S(1)} %compare_and_fusion.2, f32[512,8]{0,1:T(8,128)S(1)} %get-tuple-element.436, ...), kind=kOutput, calls=%fused_computation.9.clone.1 | convolution fusion | flops 548929536 | bytes 13008901 | tf_op jit(solution)/shard_map/while/body/eval_jaxpr/rkgn,nkd->rkgd/dot_general | solution.py:59
  182.3 2.0 fusion.39
  184.9 5.6 %fusion.37 = (f32[512,8]{0,1:T(8,128)S(1)}, f32[512,512,8]{1,0,2:T(8,128)}) fusion(pred[512,512]{0,1:T(8,128)(4,1)S(1)} %compare_and_fusion.2, bf16[512,1,8,128]{3,0,2,1:T(8,128)(2,1)S(1)} %get-tuple-element.474, bf16[4096,128]{1,0:T(8,128)(2,1)} %get-tuple-element.473, s32[]{:T(128)S(6)} %select_n.96), kind=kOutput, calls=%fused_computation.3.clone.1 | convolution fusion | flops 543158272 | bytes 9846788 | tf_op jit(solution)/shard_map/while/body/eval_jaxpr/rkgd,nkd->rkgn/dot_general | solution.py:50
  190.5 8.2 %bitcast_add_fusion.5 = f32[512,1,8,128]{0,3,2,1:T(8,128)} fusion(f32[512,1,8,128]{0,3,2,1:T(8,128)} %get-tuple-element.455, f32[512,512,8]{1,0,2:T(8,128)} %get-tuple-element.435, f32[512,8]{0,1:T(8,128)S(1)} %bitcast.92, pred[512,512]{0,1:T(8,128)(4,1)S(1)} %compare_and_fusion.2, f32[512,8]{0,1:T(8,128)S(1)} %get-tuple-element.436, ...), kind=kOutput, calls=%fused_computation.9.clone.1 | convolution fusion | flops 548929536 | bytes 13008901 | tf_op jit(solution)/shard_map/while/body/eval_jaxpr/rkgn,nkd->rkgd/dot_general | solution.py:59
  202.6 29.8 %fusion.23 = bf16[8192,512]{0,1:T(8,128)(2,1)} fusion(bf16[512,1024]{0,1:T(8,128)(2,1)S(1)} %bitcast.96, bf16[8192,1024]{1,0:T(8,128)(2,1)} %param.11), kind=kOutput, calls=%fused_computation.33 | convolution fusion | flops 8594128896 | bytes 26214400 | tf_op jit(solution)/shard_map/dot_general | solution.py:74
  232.5 167.7 %reduce-scatter.2.cloned.1.call-done = bf16[1024,512]{0,1:T(8,128)(2,1)} async-done(((bf16[8192,512]{0,1:T(8,128)(2,1)}), bf16[1024,512]{0,1:T(8,128)(2,1)}) %reduce-scatter.2.cloned.1.call-update) | async-done | bytes 1048592 | tf_op jit(solution)/shard_map/reduce_scatter | solution.py:73
  400.2 2.3 copy.43
  (124 shorter events, 17.6 us)
Async XLA Ops:
  6.5 1.9 copy-start
  6.5 36.4 %copy-start.2 = (s32[16]{0:T(128)S(1)}, s32[16]{0:T(128)}, u32[]{:S(2)}) copy-start(s32[16]{0:T(128)} %param.12) | copy-start | bytes 196
  10.6 26.7 %all-to-all-start = ((bf16[16,32,1024]{2,1,0:T(8,128)(2,1)}), bf16[16,32,1024]{2,1,0:T(8,128)(2,1)S(1)}, u32[]{:S(2)}, u32[]{:S(2)}) async-start(bf16[16,32,1024]{2,1,0:T(8,128)(2,1)} %copy.38), calls=%async_computation | async-start | bytes 2097152 | tf_op jit(solution)/shard_map/all_to_all | solution.py:98
  20.1 49.8 %all-gather.2.cloned.1.call-start = ((), (), s32[]{:S(2)}) async-start(), calls=%async_computation.3 | async-start | bytes 1114112 | tf_op jit(solution)/shard_map/all_gather | solution.py:28
  38.3 21.6 %all-to-all-start.1 = ((bf16[16,256,128]{1,2,0:T(8,128)(2,1)}), bf16[16,256,128]{1,2,0:T(8,128)(2,1)S(1)}, u32[]{:S(2)}, u32[]{:S(2)}) async-start(bf16[16,256,128]{1,2,0:T(8,128)(2,1)} %stack.2), calls=%async_computation.1 | async-start | bytes 2097152 | tf_op jit(solution)/shard_map/all_to_all | solution.py:30
  42.7 357.4 %reduce-scatter.2.cloned.1.call-start = ((), (), s32[]{:S(2)}) async-start(), calls=%async_computation.4 | async-start | bytes 9437184 | tf_op jit(solution)/shard_map/reduce_scatter | solution.py:73
  76.0 7.6 %copy-start.1 = (f32[512,512,8]{1,0,2:T(8,128)S(1)}, f32[512,512,8]{1,0,2:T(8,128)}, u32[]{:S(2)}) copy-start(f32[512,512,8]{1,0,2:T(8,128)} %get-tuple-element.435) | copy-start | bytes 25165828 | tf_op jit(solution)/shard_map/while
  91.9 8.2 %copy-start.1 = (f32[512,512,8]{1,0,2:T(8,128)S(1)}, f32[512,512,8]{1,0,2:T(8,128)}, u32[]{:S(2)}) copy-start(f32[512,512,8]{1,0,2:T(8,128)} %get-tuple-element.435) | copy-start | bytes 25165828 | tf_op jit(solution)/shard_map/while
  108.3 8.2 %copy-start.1 = (f32[512,512,8]{1,0,2:T(8,128)S(1)}, f32[512,512,8]{1,0,2:T(8,128)}, u32[]{:S(2)}) copy-start(f32[512,512,8]{1,0,2:T(8,128)} %get-tuple-element.435) | copy-start | bytes 25165828 | tf_op jit(solution)/shard_map/while
  124.8 8.2 %copy-start.1 = (f32[512,512,8]{1,0,2:T(8,128)S(1)}, f32[512,512,8]{1,0,2:T(8,128)}, u32[]{:S(2)}) copy-start(f32[512,512,8]{1,0,2:T(8,128)} %get-tuple-element.435) | copy-start | bytes 25165828 | tf_op jit(solution)/shard_map/while
  141.2 8.2 %copy-start.1 = (f32[512,512,8]{1,0,2:T(8,128)S(1)}, f32[512,512,8]{1,0,2:T(8,128)}, u32[]{:S(2)}) copy-start(f32[512,512,8]{1,0,2:T(8,128)} %get-tuple-element.435) | copy-start | bytes 25165828 | tf_op jit(solution)/shard_map/while
  157.6 8.2 %copy-start.1 = (f32[512,512,8]{1,0,2:T(8,128)S(1)}, f32[512,512,8]{1,0,2:T(8,128)}, u32[]{:S(2)}) copy-start(f32[512,512,8]{1,0,2:T(8,128)} %get-tuple-element.435) | copy-start | bytes 25165828 | tf_op jit(solution)/shard_map/while
  174.1 8.2 %copy-start.1 = (f32[512,512,8]{1,0,2:T(8,128)S(1)}, f32[512,512,8]{1,0,2:T(8,128)}, u32[]{:S(2)}) copy-start(f32[512,512,8]{1,0,2:T(8,128)} %get-tuple-element.435) | copy-start | bytes 25165828 | tf_op jit(solution)/shard_map/while
  190.5 8.2 %copy-start.1 = (f32[512,512,8]{1,0,2:T(8,128)S(1)}, f32[512,512,8]{1,0,2:T(8,128)}, u32[]{:S(2)}) copy-start(f32[512,512,8]{1,0,2:T(8,128)} %get-tuple-element.435) | copy-start | bytes 25165828 | tf_op jit(solution)/shard_map/while
Sparse Core Ops, SparseCore 0:
  23.4 46.4 all-gather.1
  232.6 167.4 reduce-scatter.1
